TPU v7x, 256 devices: a whole 4x4x8 slice. The times are simulated.
256 devices in a mesh: section: 64 (over z_hi, y, x, core), tp: 4 (over z_lo).
Axes of the slice: x: 4, y: 4, z: 8 (z_hi: 2, z_lo: 4; z = z_hi * 4 + z_lo), core: 2. Of those that a mesh axis runs over, the one named last changes fastest.
Arguments:
- param: float32 [4096, 3584], P('section', 'tp'), may hold values from -4 to 4
- moment_one: float32 [4096, 3584], P('section', 'tp'), may hold values from -2 to 2
- moment_two: float32 [4096, 3584], P('section', 'tp'), may hold values from 0.001 to 1
- proj_grad: float32 [4096, 3584], P('section', 'tp'), may hold values from -6 to 6
- embed_grad: bfloat16 [32768, 3584], P('section', 'tp'), may hold values from -6 to 6
- token_ids: int32 [32768], P('section'), may hold values from 0 to 4095, as said below
- next_ids: int32 [32768], P('section'), may hold values from 0 to 4095, as said below
Outputs:
- new_param: float32 [4096, 3584], P('section', 'tp')
- new_moment_one: float32 [4096, 3584], P('section', 'tp')
- new_moment_two: float32 [4096, 3584], P('section', 'tp')
- next_rows: bfloat16 [32768, 3584], P('section')
Inputs may be any that keep to these rules, and one draw needn't show every extreme that they name: `token_ids`: in each section index's block of 512 tokens at most 16 ids fall into any one owner's run of 64 table rows (id // 64); in every draw some owner receives exactly 16 from every block. `next_ids`: the same bound of 16 a block and an owner holds, and is reached, as for token_ids.
All inputs are finite; a program needn't handle non-finite values.
Results may differ from a plain program's by a relative error of at most 0.001.
Values may be sent and summed in bfloat16 or wider, within the bound.
No kernel may reach another device: no remote copies, remote signals or barrier semaphores. Data moves between devices by JAX's collectives and lax.ppermute only.
A program may use at most 64 MiB of HBM per device.

v0:
```python
import jax
import jax.numpy as jnp
from jax import lax
from jax.sharding import PartitionSpec as P

STEP = 1000


def slot_layout(ids, owners, cap, rows_own):
    owner = ids // rows_own
    hits = (owner[:, None] == jnp.arange(owners)[None, :]).astype(jnp.int32)
    before = jnp.cumsum(hits, axis=0) - hits
    rank = jnp.sum(before * hits, axis=1)
    return (owner * cap + rank, ids - owner * rows_own)


def on_device(param, moment_one, moment_two, proj_grad, embed_grad, token_ids, next_ids):
    rows_own, width = param.shape
    owners = lax.axis_size("section")
    tokens_here = token_ids.shape[0]
    cap = 2 * tokens_here // owners
    slot, local = slot_layout(token_ids, owners, cap, rows_own)
    outgoing = jnp.zeros((owners * cap, width), jnp.bfloat16).at[slot].set(embed_grad)
    targets = jnp.full((owners * cap,), -1, jnp.int32).at[slot].set(local)
    got_rows, got_local = (
        lax.all_to_all(
            outgoing.reshape(owners, cap, width), "section", split_axis=0, concat_axis=0, tiled=True
        ),
        lax.all_to_all(
            targets.reshape(owners, cap), "section", split_axis=0, concat_axis=0, tiled=True
        ),
    )
    select = (jnp.arange(rows_own)[:, None] == got_local.reshape(-1)[None, :]).astype(jnp.bfloat16)
    embed_sum = jnp.dot(
        select, got_rows.reshape(owners * cap, width), preferred_element_type=jnp.float32
    )
    grad = proj_grad + embed_sum
    new_moment_one = 0.9 * moment_one + 0.1 * grad
    new_moment_two = 0.999 * moment_two + 0.001 * grad * grad
    first_fix = 1.0 - 0.9**STEP
    second_fix = 1.0 - 0.999**STEP
    new_param = param - 0.01 * (new_moment_one / first_fix) / (
        jnp.sqrt(new_moment_two / second_fix) + 1e-08
    )
    table = new_param.astype(jnp.bfloat16)
    slot, local = slot_layout(next_ids, owners, cap, rows_own)
    asking = jnp.full((owners * cap,), -1, jnp.int32).at[slot].set(local).reshape(owners, cap)
    found = jnp.take(
        table,
        jnp.clip(
            lax.all_to_all(asking, "section", split_axis=0, concat_axis=0, tiled=True),
            0,
            rows_own - 1,
        ),
        axis=0,
    )
    replies = lax.all_to_all(found, "section", split_axis=0, concat_axis=0, tiled=True)
    mine = jnp.take(replies.reshape(owners * cap, width), slot, axis=0)
    next_rows = lax.all_gather(mine, "tp", axis=1, tiled=True)
    return (new_param, new_moment_one, new_moment_two, next_rows)


def solution(mesh):
    placed = (
        P("section", "tp"),
        P("section", "tp"),
        P("section", "tp"),
        P("section", "tp"),
        P("section", "tp"),
        P("section"),
        P("section"),
    )
    return jax.shard_map(
        on_device,
        mesh=mesh,
        in_specs=placed,
        out_specs=(P("section", "tp"), P("section", "tp"), P("section", "tp"), P("section", None)),
        check_vma=False,
    )
```

profile of v0, /device:TPU:1, one launch (start us, length us, event | category | flops | bytes accessed | tf_op | source)
XLA Modules:
  0.0 256.6 jit_solution(6298130976324283758)
XLA Ops:
  7.2 0.7 multiply_subtract_fusion
  7.9 1.2 reduce-window.16
  9.5 2.4 scatter_custom_fusion.2
  11.9 0.7 all_to_all.21
  12.6 15.6 %all-to-all-start.2 = ((s32[64,1,16]{2,1,0:T(1,128)}), s32[64,1,16]{2,1,0:T(1,128)S(1)}, u32[]{:S(2)}, u32[]{:S(2)}) async-start(s32[64,1,16]{2,1,0:T(1,128)} %bitcast.7), calls=%async_computation.2 | async-start | bytes 65536 | tf_op jit(solution)/shard_map/all_to_all | solution.py:51
  28.3 0.7 multiply_subtract_fusion.1
  29.0 1.2 reduce-window.14
  30.6 2.4 scatter_custom_fusion
  33.7 6.2 %all-to-all-done.2 = s32[64,1,16]{2,1,0:T(1,128)S(1)} async-done(((s32[64,1,16]{2,1,0:T(1,128)}), s32[64,1,16]{2,1,0:T(1,128)S(1)}, u32[]{:S(2)}, u32[]{:S(2)}) %all-to-all-start.2) | async-done | bytes 4128 | tf_op jit(solution)/shard_map/all_to_all | solution.py:51
  40.0 6.6 %all-to-all-start = ((s32[64,1,16]{2,1,0:T(1,128)}), s32[64,1,16]{2,1,0:T(1,128)S(1)}, u32[]{:S(2)}, u32[]{:S(2)}) async-start(s32[64,1,16]{2,1,0:T(1,128)} %bitcast.2), calls=%async_computation | async-start | bytes 65536 | tf_op jit(solution)/shard_map/all_to_all | solution.py:29
  46.5 4.6 %scatter_custom_fusion.1 = bf16[1024,896]{1,0:T(8,128)(2,1)} fusion(s32[512]{0:T(512)S(1)} %compare_select_fusion.3, bf16[512,896]{1,0:T(8,128)(2,1)} %param.11, bf16[]{:T(256)} %constant.74.clone.1), kind=kCustom, calls=%fused_computation.7 | custom fusion | bytes 1835520 | tf_op jit(solution)/shard_map/scatter | solution.py:23
  51.1 7.1 %all-to-all-done = s32[64,1,16]{2,1,0:T(1,128)S(1)} async-done(((s32[64,1,16]{2,1,0:T(1,128)}), s32[64,1,16]{2,1,0:T(1,128)S(1)}, u32[]{:S(2)}, u32[]{:S(2)}) %all-to-all-start) | async-done | bytes 4128 | tf_op jit(solution)/shard_map/all_to_all | solution.py:29
  58.3 5.8 %all-to-all-start.1 = ((bf16[64,16,896]{2,1,0:T(8,128)(2,1)}), bf16[64,16,896]{2,1,0:T(8,128)(2,1)S(1)}, u32[]{:S(2)}, u32[]{:S(2)}) async-start(bf16[64,16,896]{2,1,0:T(8,128)(2,1)} %bitcast.56), calls=%async_computation.1 | async-start | bytes 3670016 | tf_op jit(solution)/shard_map/all_to_all | solution.py:26
  64.8 0.7 reduce.7
  65.6 32.1 %all-to-all-done.1 = bf16[64,16,896]{2,1,0:T(8,128)(2,1)S(1)} async-done(((bf16[64,16,896]{2,1,0:T(8,128)(2,1)}), bf16[64,16,896]{2,1,0:T(8,128)(2,1)S(1)}, u32[]{:S(2)}, u32[]{:S(2)}) %all-to-all-start.1) | async-done | bytes 1835040 | tf_op jit(solution)/shard_map/all_to_all | solution.py:26
  97.7 1.3 fusion.20
  99.1 4.0 %gather_fusion = bf16[1024,896]{1,0:T(8,128)(2,1)S(1)} fusion(bf16[64,896]{1,0:T(8,128)(2,1)S(1)} %get-tuple-element.8, s32[1024]{0:T(1024)S(1)} %broadcast_clamp_fusion.1), kind=kCustom, calls=%fused_computation | custom fusion | bytes 3674112 | tf_op jit(solution)/shard_map/jit(_take)/gather | solution.py:48
  103.1 1.5 broadcast_select_fusion
  104.6 19.2 %all-to-all-start.3 = ((bf16[64,16,896]{2,1,0:T(8,128)(2,1)}), bf16[64,16,896]{2,1,0:T(8,128)(2,1)S(1)}, u32[]{:S(2)}, u32[]{:S(2)}) async-start(bf16[64,16,896]{2,1,0:T(8,128)(2,1)} %broadcast_select_fusion), calls=%async_computation.3 | async-start | bytes 3670016 | tf_op jit(solution)/shard_map/all_to_all | solution.py:57
  123.9 28.8 %all-to-all-done.3 = bf16[64,16,896]{2,1,0:T(8,128)(2,1)S(1)} async-done(((bf16[64,16,896]{2,1,0:T(8,128)(2,1)}), bf16[64,16,896]{2,1,0:T(8,128)(2,1)S(1)}, u32[]{:S(2)}, u32[]{:S(2)}) %all-to-all-start.3) | async-done | bytes 1835040 | tf_op jit(solution)/shard_map/all_to_all | solution.py:57
  152.7 2.0 gather_fusion.1
  154.7 1.1 broadcast_select_fusion.1
  155.9 89.8 %all-gather.2.cloned.1.call-done = bf16[512,3584]{1,0:T(8,128)(2,1)} async-done(((bf16[512,896]{1,0:T(8,128)(2,1)}), bf16[512,3584]{1,0:T(8,128)(2,1)}) %all-gather.2.cloned.1.call-update) | async-done | bytes 3670032 | tf_op jit(solution)/shard_map/all_gather | solution.py:59
  245.7 4.1 %copy.22 = bf16[512,3584]{1,0:T(8,128)(2,1)} copy(bf16[512,3584]{1,0:T(8,128)(2,1)} %all-gather.2.cloned.1.call-done) | data formatting | bytes 7340032
  (31 shorter events, 2.3 us)
Async XLA Ops:
  12.6 27.3 %all-to-all-start.2 = ((s32[64,1,16]{2,1,0:T(1,128)}), s32[64,1,16]{2,1,0:T(1,128)S(1)}, u32[]{:S(2)}, u32[]{:S(2)}) async-start(s32[64,1,16]{2,1,0:T(1,128)} %bitcast.7), calls=%async_computation.2 | async-start | bytes 65536 | tf_op jit(solution)/shard_map/all_to_all | solution.py:51
  40.0 18.3 %all-to-all-start = ((s32[64,1,16]{2,1,0:T(1,128)}), s32[64,1,16]{2,1,0:T(1,128)S(1)}, u32[]{:S(2)}, u32[]{:S(2)}) async-start(s32[64,1,16]{2,1,0:T(1,128)} %bitcast.2), calls=%async_computation | async-start | bytes 65536 | tf_op jit(solution)/shard_map/all_to_all | solution.py:29
  58.3 39.4 %copy-start = (f32[64,896]{1,0:T(8,128)S(1)}, f32[64,896]{1,0:T(8,128)}, u32[]{:S(2)}) copy-start(f32[64,896]{1,0:T(8,128)} %param.7) | copy-start | bytes 688132
  58.3 39.4 %copy-start.1 = (f32[64,896]{1,0:T(8,128)S(1)}, f32[64,896]{1,0:T(8,128)}, u32[]{:S(2)}) copy-start(f32[64,896]{1,0:T(8,128)} %param.8) | copy-start | bytes 688132
  58.3 39.4 %copy-start.2 = (f32[64,896]{1,0:T(8,128)S(1)}, f32[64,896]{1,0:T(8,128)}, u32[]{:S(2)}) copy-start(f32[64,896]{1,0:T(8,128)} %param.9) | copy-start | bytes 688132
  58.3 39.4 %copy-start.3 = (f32[64,896]{1,0:T(8,128)S(1)}, f32[64,896]{1,0:T(8,128)}, u32[]{:S(2)}) copy-start(f32[64,896]{1,0:T(8,128)} %param.10) | copy-start | bytes 688132
  58.3 39.4 %all-to-all-start.1 = ((bf16[64,16,896]{2,1,0:T(8,128)(2,1)}), bf16[64,16,896]{2,1,0:T(8,128)(2,1)S(1)}, u32[]{:S(2)}, u32[]{:S(2)}) async-start(bf16[64,16,896]{2,1,0:T(8,128)(2,1)} %bitcast.56), calls=%async_computation.1 | async-start | bytes 3670016 | tf_op jit(solution)/shard_map/all_to_all | solution.py:26
  104.6 48.0 %all-to-all-start.3 = ((bf16[64,16,896]{2,1,0:T(8,128)(2,1)}), bf16[64,16,896]{2,1,0:T(8,128)(2,1)S(1)}, u32[]{:S(2)}, u32[]{:S(2)}) async-start(bf16[64,16,896]{2,1,0:T(8,128)(2,1)} %broadcast_select_fusion), calls=%async_computation.3 | async-start | bytes 3670016 | tf_op jit(solution)/shard_map/all_to_all | solution.py:57
  123.8 121.8 %all-gather.2.cloned.1.call-start = ((), (), s32[]{:S(2)}) async-start(), calls=%async_computation.4 | async-start | bytes 4587520 | tf_op jit(solution)/shard_map/all_gather | solution.py:59
Sparse Core Ops, SparseCore 0:
  156.0 89.6 all-gather.1
where the time goes:
time: 257 us
  waiting for transfers between devices  164 us (64%)
  starting transfers between devices  47.2 us (18%)
  local copies, waits for them, and re-layouts  22.2 us (9%)
  between operations  14.2 us (6%)
  other arithmetic  7.61 us (3%)
    all_gather x1, waiting for transfers between devices, on_device(): next_rows = lax.all_gather(mine, 'tp', axis=1, tiled=True)  89.8 us
    all_to_all x1, waiting for transfers between devices, on_device(): lax.all_to_all(outgoing.reshape(owners, cap, width), 'section', split_axi...  32.1 us
    all_to_all x1, waiting for transfers between devices, on_device(): lax.all_to_all(found, 'section', split_axis=0, concat_axis=0, tiled=True)  28.8 us
    all_to_all x1, starting transfers between devices, on_device(): lax.all_to_all(found, 'section', split_axis=0, concat_axis=0, tiled=True)  19.2 us
    all_to_all x1, starting transfers between devices, on_device(): lax.all_to_all(asking, 'section', split_axis=0, concat_axis=0, tiled=True)  15.6 us
    all_to_all x1, waiting for transfers between devices, on_device(): lax.all_to_all(targets.reshape(owners, cap), 'section', split_axis=0, con...  7.12 us
    all_to_all x1, starting transfers between devices, on_device(): lax.all_to_all(targets.reshape(owners, cap), 'section', split_axis=0, con...  6.58 us
    all_to_all x1, waiting for transfers between devices, on_device(): lax.all_to_all(asking, 'section', split_axis=0, concat_axis=0, tiled=True)  6.23 us
  transfers between devices with their start and end apart: 5, of which 5 were waited for; matrix products, arithmetic and copies ran while one was open for 4% of the time, Pallas kernels for 0%

commit v1 on v0

--- a/solution.py
+++ b/solution.py
@@ -56,7 +56,9 @@
     )
     replies = lax.all_to_all(found, "section", split_axis=0, concat_axis=0, tiled=True)
     mine = jnp.take(replies.reshape(owners * cap, width), slot, axis=0)
-    next_rows = lax.all_gather(mine, "tp", axis=1, tiled=True)
+    next_rows = jnp.concatenate(
+        lax.all_to_all(jnp.stack([mine] * lax.axis_size("tp")), "tp", 0, 0), axis=1
+    )
     return (new_param, new_moment_one, new_moment_two, next_rows)
 
 

time: 257 us -> 265 us (1.031)
  blocking collectives: 0 us -> 104 us
  waiting for transfers between devices: 164 us -> 74.3 us
  between operations: 14.2 us -> 0.8 us
  local copies, waits for them, and re-layouts: 22.2 us -> 30.2 us
    all_to_all x0 -> x1, blocking collectives: none -> 104 us  [on_device(): lax.all_to_all(jnp.stack([mine] * lax.axis_size('tp')), 'tp', 0, 0)]
    all_gather x1 -> x0, waiting for transfers between devices: 89.8 us -> none  [on_device(): next_rows = lax.all_gather(mine, 'tp', axis=1, tiled=True)]
    all_to_all x0 -> x1, local copies, waits for them, and re-layouts: none -> 5.94 us  [on_device(): lax.all_to_all(jnp.stack([mine] * lax.axis_size('tp')), 'tp', 0, 0)]
  transfers between devices with their start and end apart: 5 -> 4, of which waited for: 5 -> 4; matrix products, arithmetic and copies ran while one was open for 4% -> 4% of each run, Pallas kernels for 0% -> 0%
where the time goes in v1:
time: 265 us; the launch traced here: 264 us
  blocking collectives  104 us (39%)
  waiting for transfers between devices  74.3 us (28%)
  starting transfers between devices  47.2 us (18%)
  local copies, waits for them, and re-layouts  30.2 us (11%)
  other arithmetic  6.68 us (3%)
    all_to_all x1, blocking collectives, on_device(): lax.all_to_all(jnp.stack([mine] * lax.axis_size('tp')), 'tp', 0, 0)  104 us
    all_to_all x1, waiting for transfers between devices, on_device(): lax.all_to_all(outgoing.reshape(owners, cap, width), 'section', split_axi...  32.1 us
    all_to_all x1, waiting for transfers between devices, on_device(): lax.all_to_all(found, 'section', split_axis=0, concat_axis=0, tiled=True)  28.9 us
    all_to_all x1, starting transfers between devices, on_device(): lax.all_to_all(found, 'section', split_axis=0, concat_axis=0, tiled=True)  19.2 us
    all_to_all x1, starting transfers between devices, on_device(): lax.all_to_all(asking, 'section', split_axis=0, concat_axis=0, tiled=True)  15.6 us
    all_to_all x1, waiting for transfers between devices, on_device(): lax.all_to_all(targets.reshape(owners, cap), 'section', split_axis=0, con...  7.12 us
    all_to_all x1, starting transfers between devices, on_device(): lax.all_to_all(targets.reshape(owners, cap), 'section', split_axis=0, con...  6.58 us
    all_to_all x1, waiting for transfers between devices, on_device(): lax.all_to_all(asking, 'section', split_axis=0, concat_axis=0, tiled=True)  6.23 us
  transfers between devices with their start and end apart: 4, of which 4 were waited for; matrix products, arithmetic and copies ran while one was open for 4% of the time, Pallas kernels for 0%

profile of v1, /device:TPU:1, one launch (start us, length us, event | category | flops | bytes accessed | tf_op | source)
XLA Modules:
  0.0 264.2 jit_solution(14296244771460653751)
XLA Ops:
  0.6 0.7 multiply_subtract_fusion
  1.3 1.2 reduce-window.16
  3.0 2.4 scatter_custom_fusion.2
  5.4 0.7 all_to_all.24
  6.1 15.6 %all-to-all-start.2 = ((s32[64,1,16]{2,1,0:T(1,128)}), s32[64,1,16]{2,1,0:T(1,128)S(1)}, u32[]{:S(2)}, u32[]{:S(2)}) async-start(s32[64,1,16]{2,1,0:T(1,128)} %bitcast.7), calls=%async_computation.2 | async-start | bytes 65536 | tf_op jit(solution)/shard_map/all_to_all | solution.py:51
  21.7 0.7 multiply_subtract_fusion.1
  22.4 1.2 reduce-window.14
  24.0 2.4 scatter_custom_fusion
  27.2 6.2 %all-to-all-done.2 = s32[64,1,16]{2,1,0:T(1,128)S(1)} async-done(((s32[64,1,16]{2,1,0:T(1,128)}), s32[64,1,16]{2,1,0:T(1,128)S(1)}, u32[]{:S(2)}, u32[]{:S(2)}) %all-to-all-start.2) | async-done | bytes 4128 | tf_op jit(solution)/shard_map/all_to_all | solution.py:51
  33.4 6.6 %all-to-all-start = ((s32[64,1,16]{2,1,0:T(1,128)}), s32[64,1,16]{2,1,0:T(1,128)S(1)}, u32[]{:S(2)}, u32[]{:S(2)}) async-start(s32[64,1,16]{2,1,0:T(1,128)} %bitcast.2), calls=%async_computation | async-start | bytes 65536 | tf_op jit(solution)/shard_map/all_to_all | solution.py:29
  40.0 4.6 %scatter_custom_fusion.1 = bf16[1024,896]{1,0:T(8,128)(2,1)} fusion(s32[512]{0:T(512)S(1)} %compare_select_fusion.3, bf16[512,896]{1,0:T(8,128)(2,1)} %param.11, bf16[]{:T(256)} %constant.74.clone.1), kind=kCustom, calls=%fused_computation.7 | custom fusion | bytes 1835520 | tf_op jit(solution)/shard_map/scatter | solution.py:23
  44.6 7.1 %all-to-all-done = s32[64,1,16]{2,1,0:T(1,128)S(1)} async-done(((s32[64,1,16]{2,1,0:T(1,128)}), s32[64,1,16]{2,1,0:T(1,128)S(1)}, u32[]{:S(2)}, u32[]{:S(2)}) %all-to-all-start) | async-done | bytes 4128 | tf_op jit(solution)/shard_map/all_to_all | solution.py:29
  51.7 5.8 %all-to-all-start.1 = ((bf16[64,16,896]{2,1,0:T(8,128)(2,1)}), bf16[64,16,896]{2,1,0:T(8,128)(2,1)S(1)}, u32[]{:S(2)}, u32[]{:S(2)}) async-start(bf16[64,16,896]{2,1,0:T(8,128)(2,1)} %bitcast.60), calls=%async_computation.1 | async-start | bytes 3670016 | tf_op jit(solution)/shard_map/all_to_all | solution.py:26
  58.2 0.7 reduce.7
  59.1 32.1 %all-to-all-done.1 = bf16[64,16,896]{2,1,0:T(8,128)(2,1)S(1)} async-done(((bf16[64,16,896]{2,1,0:T(8,128)(2,1)}), bf16[64,16,896]{2,1,0:T(8,128)(2,1)S(1)}, u32[]{:S(2)}, u32[]{:S(2)}) %all-to-all-start.1) | async-done | bytes 1835040 | tf_op jit(solution)/shard_map/all_to_all | solution.py:26
  91.2 1.3 fusion.20
  92.5 4.0 %gather_fusion = bf16[1024,896]{1,0:T(8,128)(2,1)S(1)} fusion(bf16[64,896]{1,0:T(8,128)(2,1)S(1)} %get-tuple-element.12, s32[1024]{0:T(1024)S(1)} %broadcast_clamp_fusion.1), kind=kCustom, calls=%fused_computation | custom fusion | bytes 3674112 | tf_op jit(solution)/shard_map/jit(_take)/gather | solution.py:48
  96.6 1.5 broadcast_select_fusion
  98.1 19.2 %all-to-all-start.3 = ((bf16[64,16,896]{2,1,0:T(8,128)(2,1)}), bf16[64,16,896]{2,1,0:T(8,128)(2,1)S(1)}, u32[]{:S(2)}, u32[]{:S(2)}) async-start(bf16[64,16,896]{2,1,0:T(8,128)(2,1)} %broadcast_select_fusion), calls=%async_computation.3 | async-start | bytes 3670016 | tf_op jit(solution)/shard_map/all_to_all | solution.py:57
  117.3 28.9 %all-to-all-done.3 = bf16[64,16,896]{2,1,0:T(8,128)(2,1)S(1)} async-done(((bf16[64,16,896]{2,1,0:T(8,128)(2,1)}), bf16[64,16,896]{2,1,0:T(8,128)(2,1)S(1)}, u32[]{:S(2)}, u32[]{:S(2)}) %all-to-all-start.3) | async-done | bytes 1835040 | tf_op jit(solution)/shard_map/all_to_all | solution.py:57
  146.1 2.0 gather_fusion.1
  148.7 103.7 %all_to_all.33 = bf16[4,512,896]{2,1,0:T(8,128)(2,1)} all-to-all(bf16[4,512,896]{2,1,0:T(8,128)(2,1)S(1)} %stack.2), channel_id=1, replica_groups=mesh['section'=64,'tp'=4] {'tp'}, dimensions={0} | all-to-all | bytes 7340032 | tf_op jit(solution)/shard_map/all_to_all | solution.py:60
  252.3 5.9 %copy.21 = bf16[4,512,896]{1,2,0:T(8,128)(2,1)} copy(bf16[4,512,896]{2,1,0:T(8,128)(2,1)} %all_to_all.33) | data formatting | bytes 7340032 | tf_op jit(solution)/shard_map/all_to_all | solution.py:60
  258.3 5.9 %copy.22 = bf16[512,3584]{1,0:T(8,128)(2,1)} copy(bf16[512,3584]{0,1:T(8,128)(2,1)} %bitcast.58) | data formatting | bytes 7340032
  (31 shorter events, 2.7 us)
Async XLA Ops:
  6.1 27.3 %all-to-all-start.2 = ((s32[64,1,16]{2,1,0:T(1,128)}), s32[64,1,16]{2,1,0:T(1,128)S(1)}, u32[]{:S(2)}, u32[]{:S(2)}) async-start(s32[64,1,16]{2,1,0:T(1,128)} %bitcast.7), calls=%async_computation.2 | async-start | bytes 65536 | tf_op jit(solution)/shard_map/all_to_all | solution.py:51
  33.4 18.3 %all-to-all-start = ((s32[64,1,16]{2,1,0:T(1,128)}), s32[64,1,16]{2,1,0:T(1,128)S(1)}, u32[]{:S(2)}, u32[]{:S(2)}) async-start(s32[64,1,16]{2,1,0:T(1,128)} %bitcast.2), calls=%async_computation | async-start | bytes 65536 | tf_op jit(solution)/shard_map/all_to_all | solution.py:29
  51.7 39.4 %copy-start = (f32[64,896]{1,0:T(8,128)S(1)}, f32[64,896]{1,0:T(8,128)}, u32[]{:S(2)}) copy-start(f32[64,896]{1,0:T(8,128)} %param.7) | copy-start | bytes 688132
  51.7 39.4 %copy-start.1 = (f32[64,896]{1,0:T(8,128)S(1)}, f32[64,896]{1,0:T(8,128)}, u32[]{:S(2)}) copy-start(f32[64,896]{1,0:T(8,128)} %param.8) | copy-start | bytes 688132
  51.7 39.4 %copy-start.2 = (f32[64,896]{1,0:T(8,128)S(1)}, f32[64,896]{1,0:T(8,128)}, u32[]{:S(2)}) copy-start(f32[64,896]{1,0:T(8,128)} %param.9) | copy-start | bytes 688132
  51.7 39.4 %copy-start.3 = (f32[64,896]{1,0:T(8,128)S(1)}, f32[64,896]{1,0:T(8,128)}, u32[]{:S(2)}) copy-start(f32[64,896]{1,0:T(8,128)} %param.10) | copy-start | bytes 688132
  51.7 39.4 %all-to-all-start.1 = ((bf16[64,16,896]{2,1,0:T(8,128)(2,1)}), bf16[64,16,896]{2,1,0:T(8,128)(2,1)S(1)}, u32[]{:S(2)}, u32[]{:S(2)}) async-start(bf16[64,16,896]{2,1,0:T(8,128)(2,1)} %bitcast.60), calls=%async_computation.1 | async-start | bytes 3670016 | tf_op jit(solution)/shard_map/all_to_all | solution.py:26
  98.1 48.0 %all-to-all-start.3 = ((bf16[64,16,896]{2,1,0:T(8,128)(2,1)}), bf16[64,16,896]{2,1,0:T(8,128)(2,1)S(1)}, u32[]{:S(2)}, u32[]{:S(2)}) async-start(bf16[64,16,896]{2,1,0:T(8,128)(2,1)} %broadcast_select_fusion), calls=%async_computation.3 | async-start | bytes 3670016 | tf_op jit(solution)/shard_map/all_to_all | solution.py:57
